TPU v7x, 32 devices: a whole 2x2x4 slice. The times are simulated.
32 devices in a mesh: grp: 2 (over x), blk: 16 (over z, y, core).
Axes of the slice: x: 2, y: 2, z: 4, core: 2. Of those that a mesh axis runs over, the one named last changes fastest.
Arguments:
- sketch: bfloat16 [256, 131072], P(None, 'blk'), may hold values from -3 to 3
- leaf_maps: bfloat16 [2, 16, 256, 256], P('grp', 'blk')
- mix_maps: bfloat16 [2, 64, 16, 16], P('grp', 'blk')
Outputs:
- sketch_update: bfloat16 [256, 131072], P('grp', 'blk')
All inputs are finite; a program needn't handle non-finite values.
Results may differ from a plain program's by a relative error of at most 0.015.
Values may be sent and summed in bfloat16 or wider, within the bound.
A program may use at most 64 MiB of HBM per device.

v0:
```python
import jax
import jax.numpy as jnp
from jax import lax
from jax.sharding import PartitionSpec as P


def apply_section(current, leaf_map, mixing):
    columns, leaves, sub_rows = current.shape
    blocks = mixing.shape[1]
    low_part = mixing.shape[0]
    paired = jnp.dot(
        current.reshape(columns * leaves // 2, 2 * sub_rows),
        leaf_map,
        preferred_element_type=jnp.float32,
    ).astype(jnp.bfloat16)
    paired = paired.reshape(columns, blocks, low_part, sub_rows)
    result = jnp.einsum(
        "lhk,rklb->rhlb", mixing, paired, preferred_element_type=jnp.float32
    ).astype(jnp.bfloat16)
    return lax.all_to_all(
        result.reshape(columns, leaves, sub_rows), "blk", split_axis=1, concat_axis=1, tiled=True
    )


def on_device(sketch, leaf_maps, mix_maps):
    groups = lax.axis_size("grp")
    group_index = lax.axis_index("grp")
    total_cols, rows_dev = sketch.shape
    sub_rows = leaf_maps.shape[2] // 2
    leaves = rows_dev // sub_rows
    own_cols = total_cols // groups
    every_leaf, every_mix = (
        lax.all_gather(leaf_maps, "grp", axis=0, tiled=True),
        lax.all_gather(mix_maps, "grp", axis=0, tiled=True),
    )
    current = lax.dynamic_slice_in_dim(sketch, group_index * own_cols, own_cols, 0).reshape(
        own_cols, leaves, sub_rows
    )

    def advance_all(section_index, current):
        return apply_section(current, every_leaf[section_index, 0], every_mix[section_index])

    current = lax.fori_loop(0, groups, advance_all, current)
    return current.reshape(own_cols, rows_dev)


def solution(mesh):
    placed = (P(None, "blk"), P("grp", "blk", None, None), P("grp", "blk", None, None))
    return jax.shard_map(
        on_device, mesh=mesh, in_specs=placed, out_specs=P("grp", "blk"), check_vma=False
    )
```

profile of v0, /device:TPU:15, one launch (start us, length us, event | category | flops | bytes accessed | tf_op | source)
XLA Modules:
  0.0 160.7 jit_solution(9333081390454217977)
XLA Ops:
  0.0 3.5 %all_gather.7 = bf16[2,4,16,16]{3,2,1,0:T(8,128)(2,1)S(1)} all-gather(bf16[1,4,16,16]{3,2,1,0:T(8,128)(2,1)} %param.7), channel_id=1, replica_groups=mesh['grp'=2,'blk'=16] {'grp'}, dimensions={0}, use_global_device_ids=true | all-gather | bytes 6144 | tf_op jit(solution)/shard_map/all_gather | solution.py:34
  3.5 4.7 %all_gather.6 = bf16[2,1,256,256]{3,2,1,0:T(8,128)(2,1)S(1)} all-gather(bf16[1,1,256,256]{3,2,1,0:T(8,128)(2,1)} %param.6), channel_id=1, replica_groups=mesh['grp'=2,'blk'=16] {'grp'}, dimensions={0}, use_global_device_ids=true | all-gather | bytes 393216 | tf_op jit(solution)/shard_map/all_gather | solution.py:33
  8.1 1.7 %constant_dynamic-slice_fusion = bf16[128,8192]{1,0:T(8,128)(2,1)S(1)} fusion(bf16[256,8192]{1,0:T(8,128)(2,1)} %param.5, s32[]{:T(128)S(6)} %select_n.9), kind=kLoop, calls=%fused_computation.12 | loop fusion | bytes 4194308 | tf_op jit(solution)/shard_map/dynamic_slice | solution.py:36
  9.9 2.4 %copy.23 = bf16[128,8192]{0,1:T(8,128)(2,1)} copy(bf16[128,8192]{1,0:T(8,128)(2,1)S(1)} %constant_dynamic-slice_fusion) | data formatting | bytes 4194304
  12.3 4.1 %copy.20 = bf16[128,64,128]{2,0,1:T(8,128)(2,1)} copy(bf16[128,64,128]{0,2,1:T(8,128)(2,1)} %bitcast.33) | data formatting | bytes 4194304 | tf_op jit(solution)/shard_map/while | solution.py:43
  16.4 141.2 %while.13 = (s32[]{:T(128)}, bf16[128,64,128]{2,0,1:T(8,128)(2,1)}, bf16[2,1,256,256]{3,2,1,0:T(8,128)(2,1)S(1)}, bf16[2,4,16,16]{3,2,1,0:T(8,128)(2,1)S(1)}, s32[]{:T(128)}) while((s32[]{:T(128)}, bf16[128,64,128]{2,0,1:T(8,128)(2,1)}, bf16[2,1,256,256]{3,2,1,0:T(8,128)(2,1)S(1)}, bf16[2,4,16,16]{3,2,1,0:T(8,128)(2,1)S(1)}, s32[]{:T(128)}) %tuple.30), condition=%wide.region_1.0_spmd, body=%wide.region_0.0_spmd.sunk | while | flops 572522496 | bytes 44187776 | solution.py:43
  16.4 2.9 %copy.35 = bf16[128,64,128]{2,1,0:T(8,128)(2,1)S(1)} copy(bf16[128,64,128]{2,0,1:T(8,128)(2,1)} %get-tuple-element.132) | data formatting | bytes 4194304 | tf_op jit(solution)/shard_map
  19.3 2.1 %reshape.32 = bf16[4096,256]{1,0:T(8,128)(2,1)} reshape(bf16[128,64,128]{2,1,0:T(8,128)(2,1)S(1)} %copy.35) | data formatting | bytes 4194304 | tf_op jit(solution)/shard_map/while/body/eval_jaxpr/reshape | solution.py:12
  21.5 2.4 %fusion.22 = bf16[4096,256]{0,1:T(8,128)(2,1)S(1)} fusion(bf16[4096,256]{1,0:T(8,128)(2,1)} %reshape.32, bf16[2,1,256,256]{3,2,1,0:T(8,128)(2,1)S(1)} %get-tuple-element.138, s32[]{:T(128)} %get-tuple-element.131), kind=kOutput, calls=%fused_computation.1.clone.1 | convolution fusion | flops 537919488 | bytes 4325380 | tf_op jit(solution)/shard_map/while/body/eval_jaxpr/dot_general | solution.py:11
  23.8 2.5 %copy.36 = bf16[4096,256]{1,0:T(8,128)(2,1)} copy(bf16[4096,256]{0,1:T(8,128)(2,1)S(1)} %fusion.22) | data formatting | bytes 4194304 | tf_op jit(solution)/shard_map/while/body/eval_jaxpr/convert_element_type | solution.py:15
  26.3 2.5 %reshape.33 = bf16[128,16,4,128]{3,2,1,0:T(4,128)(2,1)S(1)} reshape(bf16[4096,256]{1,0:T(8,128)(2,1)} %copy.36) | data formatting | bytes 4194304 | tf_op jit(solution)/shard_map/while/body/eval_jaxpr/reshape | solution.py:16
  28.8 0.7 convert_bitcast_fusion.2
  29.5 1.9 %copy.37 = bf16[128,16,4,128]{3,0,2,1:T(8,128)(2,1)} copy(bf16[128,16,4,128]{3,1,0,2:T(8,128)(2,1)S(1)} %convert_bitcast_fusion.2) | data formatting | bytes 4194304 | tf_op jit(solution)/shard_map/while/body/eval_jaxpr/convert_element_type | solution.py:19
  31.4 8.8 %all-to-all-start = ((bf16[128,64,128]{2,0,1:T(8,128)(2,1)}), bf16[128,64,128]{2,0,1:T(8,128)(2,1)S(1)}, u32[]{:S(2)}, u32[]{:S(2)}) async-start(bf16[128,64,128]{2,0,1:T(8,128)(2,1)} %bitcast.32), calls=%async_computation | async-start | bytes 4194304 | tf_op jit(solution)/shard_map/while/body/eval_jaxpr/all_to_all | solution.py:20
  40.2 47.4 %all-to-all-done = bf16[128,64,128]{2,0,1:T(8,128)(2,1)S(1)} async-done(((bf16[128,64,128]{2,0,1:T(8,128)(2,1)}), bf16[128,64,128]{2,0,1:T(8,128)(2,1)S(1)}, u32[]{:S(2)}, u32[]{:S(2)}) %all-to-all-start) | async-done | bytes 2097184 | tf_op jit(solution)/shard_map/while/body/eval_jaxpr/all_to_all | solution.py:20
  87.6 0.0 copy-start
  87.6 1.3 copy-done
  89.0 2.9 %copy.35 = bf16[128,64,128]{2,1,0:T(8,128)(2,1)S(1)} copy(bf16[128,64,128]{2,0,1:T(8,128)(2,1)} %get-tuple-element.132) | data formatting | bytes 4194304 | tf_op jit(solution)/shard_map
  91.9 2.1 %reshape.32 = bf16[4096,256]{1,0:T(8,128)(2,1)} reshape(bf16[128,64,128]{2,1,0:T(8,128)(2,1)S(1)} %copy.35) | data formatting | bytes 4194304 | tf_op jit(solution)/shard_map/while/body/eval_jaxpr/reshape | solution.py:12
  94.0 2.4 %fusion.22 = bf16[4096,256]{0,1:T(8,128)(2,1)S(1)} fusion(bf16[4096,256]{1,0:T(8,128)(2,1)} %reshape.32, bf16[2,1,256,256]{3,2,1,0:T(8,128)(2,1)S(1)} %get-tuple-element.138, s32[]{:T(128)} %get-tuple-element.131), kind=kOutput, calls=%fused_computation.1.clone.1 | convolution fusion | flops 537919488 | bytes 4325380 | tf_op jit(solution)/shard_map/while/body/eval_jaxpr/dot_general | solution.py:11
  96.4 2.5 %copy.36 = bf16[4096,256]{1,0:T(8,128)(2,1)} copy(bf16[4096,256]{0,1:T(8,128)(2,1)S(1)} %fusion.22) | data formatting | bytes 4194304 | tf_op jit(solution)/shard_map/while/body/eval_jaxpr/convert_element_type | solution.py:15
  98.9 2.5 %reshape.33 = bf16[128,16,4,128]{3,2,1,0:T(4,128)(2,1)S(1)} reshape(bf16[4096,256]{1,0:T(8,128)(2,1)} %copy.36) | data formatting | bytes 4194304 | tf_op jit(solution)/shard_map/while/body/eval_jaxpr/reshape | solution.py:16
  101.4 0.7 convert_bitcast_fusion.2
  102.1 1.9 %copy.37 = bf16[128,16,4,128]{3,0,2,1:T(8,128)(2,1)} copy(bf16[128,16,4,128]{3,1,0,2:T(8,128)(2,1)S(1)} %convert_bitcast_fusion.2) | data formatting | bytes 4194304 | tf_op jit(solution)/shard_map/while/body/eval_jaxpr/convert_element_type | solution.py:19
  104.0 4.8 %all-to-all-start = ((bf16[128,64,128]{2,0,1:T(8,128)(2,1)}), bf16[128,64,128]{2,0,1:T(8,128)(2,1)S(1)}, u32[]{:S(2)}, u32[]{:S(2)}) async-start(bf16[128,64,128]{2,0,1:T(8,128)(2,1)} %bitcast.32), calls=%async_computation | async-start | bytes 4194304 | tf_op jit(solution)/shard_map/while/body/eval_jaxpr/all_to_all | solution.py:20
  108.8 47.4 %all-to-all-done = bf16[128,64,128]{2,0,1:T(8,128)(2,1)S(1)} async-done(((bf16[128,64,128]{2,0,1:T(8,128)(2,1)}), bf16[128,64,128]{2,0,1:T(8,128)(2,1)S(1)}, u32[]{:S(2)}, u32[]{:S(2)}) %all-to-all-start) | async-done | bytes 2097184 | tf_op jit(solution)/shard_map/while/body/eval_jaxpr/all_to_all | solution.py:20
  156.2 0.0 copy-start
  156.2 1.3 copy-done
  157.5 3.2 %copy_bitcast_fusion = bf16[128,8192]{1,0:T(8,128)(2,1)} fusion(bf16[128,64,128]{2,0,1:T(8,128)(2,1)} %get-tuple-element.84), kind=kLoop, calls=%fused_computation.11 | loop fusion | bytes 4194304 | tf_op jit(solution)/shard_map/reshape | solution.py:44
Async XLA Ops:
  31.4 56.3 %all-to-all-start = ((bf16[128,64,128]{2,0,1:T(8,128)(2,1)}), bf16[128,64,128]{2,0,1:T(8,128)(2,1)S(1)}, u32[]{:S(2)}, u32[]{:S(2)}) async-start(bf16[128,64,128]{2,0,1:T(8,128)(2,1)} %bitcast.32), calls=%async_computation | async-start | bytes 4194304 | tf_op jit(solution)/shard_map/while/body/eval_jaxpr/all_to_all | solution.py:20
  87.6 1.3 copy-start
  104.0 52.2 %all-to-all-start = ((bf16[128,64,128]{2,0,1:T(8,128)(2,1)}), bf16[128,64,128]{2,0,1:T(8,128)(2,1)S(1)}, u32[]{:S(2)}, u32[]{:S(2)}) async-start(bf16[128,64,128]{2,0,1:T(8,128)(2,1)} %bitcast.32), calls=%async_computation | async-start | bytes 4194304 | tf_op jit(solution)/shard_map/while/body/eval_jaxpr/all_to_all | solution.py:20
  156.2 1.3 copy-start
where the time goes:
time: 161 us
  waiting for transfers between devices  94.8 us (59%)
  local copies, waits for them, and re-layouts  38 us (24%)
  starting transfers between devices  13.6 us (8%)
  blocking collectives  8.13 us (5%)
  matrix products  6.09 us (4%)
    all_to_all x2, waiting for transfers between devices, apply_section(): lax.all_to_all(result.reshape(columns, leaves, sub_rows), 'blk', split_ax...  94.8 us
    all_to_all x2, starting transfers between devices, apply_section(): lax.all_to_all(result.reshape(columns, leaves, sub_rows), 'blk', split_ax...  13.6 us
    another operation x2, local copies, waits for them, and re-layouts  5.89 us
    reshape x2, local copies, waits for them, and re-layouts, apply_section(): paired = paired.reshape(columns, blocks, low_part, sub_rows)  5.09 us
    convert_element_type x2, local copies, waits for them, and re-layouts, apply_section(): paired = jnp.dot(current.reshape(columns * leaves // 2, 2 * sub_rows), le...  4.91 us
    dot_general x2, matrix products, apply_section(): jnp.dot(current.reshape(columns * leaves // 2, 2 * sub_rows), leaf_map, p...  4.71 us
    all_gather x1, blocking collectives, on_device(): lax.all_gather(leaf_maps, 'grp', axis=0, tiled=True)  4.68 us
    reshape x2, local copies, waits for them, and re-layouts, apply_section(): current.reshape(columns * leaves // 2, 2 * sub_rows)  4.28 us
  transfers between devices with their start and end apart: 2, of which 2 were waited for; matrix products, arithmetic and copies ran while one was open for 0% of the time, Pallas kernels for 0%

commit v1 on v0

v1 whole, which is shorter than its diff:
```python
import functools

import jax
import jax.numpy as jnp
from jax import lax
from jax.experimental import pallas as pl
from jax.experimental.pallas import tpu as pltpu
from jax.sharding import PartitionSpec as P

MESH = pl.DeviceIdType.MESH
TILE = 16


def chain_kernel(
    groups, blocks, sketch_ref, leaf_in, mix_in, out_ref,
    x_vm, send, recv, half, leaf_all, mix_all, weights,
    x_sem, send_sem, recv_sem, leaf_send, leaf_recv, mix_send, mix_recv,
):
    grp = lax.axis_index("grp")
    blk = lax.axis_index("blk")
    chunks, rows, row_len = x_vm.shape
    sub = leaf_in.shape[0] // 2
    leaves = row_len // sub
    low = leaves // blocks
    wide = low * sub
    tiles = rows // TILE

    barrier = pltpu.get_barrier_semaphore()
    for step in range(1, blocks):
        pl.semaphore_signal(
            barrier, inc=1, device_id={"blk": lax.rem(blk + step, blocks)}, device_id_type=MESH
        )
    for step in range(1, groups):
        pl.semaphore_signal(
            barrier, inc=1, device_id={"grp": lax.rem(grp + step, groups)}, device_id_type=MESH
        )

    def load(chunk):
        start = pl.multiple_of(grp * (chunks * rows) + chunk * rows, TILE)
        return pltpu.make_async_copy(
            sketch_ref.at[pl.ds(start, rows), :], x_vm.at[chunk], x_sem.at[chunk]
        )

    for chunk in range(chunks):
        load(chunk).start()

    pl.semaphore_wait(barrier, blocks - 1 + groups - 1)

    def factor_copies(step):
        partner = lax.rem(grp + step, groups)
        return (
            pltpu.make_async_remote_copy(
                leaf_in, leaf_all.at[grp], leaf_send.at[step], leaf_recv.at[step],
                device_id={"grp": partner}, device_id_type=MESH),
            pltpu.make_async_remote_copy(
                mix_in, mix_all.at[grp], mix_send.at[step], mix_recv.at[step],
                device_id={"grp": partner}, device_id_type=MESH),
        )

    for step in range(1, groups):
        for copy in factor_copies(step):
            copy.start()
    leaf_all[grp] = leaf_in[...]
    mix_all[grp] = mix_in[...]
    for step in range(1, groups):
        for copy in factor_copies(step):
            copy.wait()

    big = blocks * TILE
    spread = (
        lax.broadcasted_iota(jnp.int32, (big, blocks), 0) // TILE
        == lax.broadcasted_iota(jnp.int32, (big, blocks), 1)
    ).astype(jnp.bfloat16)
    same = (
        lax.broadcasted_iota(jnp.int32, (big, big), 0) % TILE
        == lax.broadcasted_iota(jnp.int32, (big, big), 1) % TILE
    )

    def build_weights(section):
        for l in range(low):
            mix = mix_all[section, pl.ds(l * blocks, blocks), :]
            tall = jnp.dot(spread, mix, preferred_element_type=jnp.float32).astype(jnp.bfloat16)
            full = lax.dot_general(
                tall, spread, (((1,), (1,)), ((), ())), preferred_element_type=jnp.float32)
            weights[l] = jnp.where(same, full, 0.0).astype(jnp.bfloat16)

    order = sorted(range(1, blocks), key=lambda step: (abs(step - blocks // 2), step))

    for section in range(groups):
        last = section == groups - 1
        build_weights(section)

        @pl.loop(0, chunks)
        def _(chunk):
            if section == 0:
                load(chunk).wait()
            else:
                arrived = recv.at[section - 1, chunk]
                pltpu.make_async_copy(arrived, arrived, recv_sem.at[section - 1, chunk]).wait()

            def piece(leaf):
                if section == 0:
                    return x_vm[chunk, :, pl.ds(leaf * sub, sub)]
                return recv[section - 1, chunk, leaf // low, :, pl.ds(leaf % low * sub, sub)]

            leaf_map = leaf_all[section]
            per = min(leaves // 2, max(1, 256 // rows))
            for first in range(0, leaves // 2, per):
                lhs = jnp.concatenate(
                    [jnp.concatenate([piece(2 * m), piece(2 * m + 1)], axis=1)
                     for m in range(first, first + per)], axis=0)
                product = jnp.dot(
                    lhs, leaf_map, preferred_element_type=jnp.float32).astype(jnp.bfloat16)
                for i in range(per):
                    for j in range(2):
                        half[2 * (first + i) + j] = product[
                            i * rows:(i + 1) * rows, j * sub:(j + 1) * sub]

            for l in range(low):
                rhs = jnp.concatenate(
                    [jnp.concatenate(
                        [half[k * low + l, pl.ds(t * TILE, TILE), :] for t in range(tiles)], axis=1)
                     for k in range(blocks)], axis=0)
                mixed = jnp.dot(
                    weights[l], rhs, preferred_element_type=jnp.float32).astype(jnp.bfloat16)
                for h in range(blocks):
                    for t in range(tiles):
                        send[section, chunk, h, pl.ds(t * TILE, TILE), pl.ds(l * sub, sub)] = mixed[
                            h * TILE:(h + 1) * TILE, t * sub:(t + 1) * sub]

            if last:
                place = out_ref.at[
                    pl.ds(pl.multiple_of(chunk * rows, TILE), rows),
                    pl.ds(pl.multiple_of(blk * wide, sub), wide)]
            else:
                place = recv.at[section, chunk, blk]
            for step in order:
                target = lax.rem(blk + step, blocks)
                pltpu.make_async_remote_copy(
                    send.at[section, chunk, target], place,
                    send_sem.at[section, chunk], recv_sem.at[section, chunk],
                    device_id={"blk": target}, device_id_type=MESH).start()
            pltpu.make_async_copy(
                send.at[section, chunk, blk], place, recv_sem.at[section, chunk]).start()

    @pl.loop(0, chunks)
    def _(chunk):
        arrived = out_ref.at[pl.ds(pl.multiple_of(chunk * rows, TILE), rows), :]
        pltpu.make_async_copy(arrived, arrived, recv_sem.at[groups - 1, chunk]).wait()
        for section in range(groups):
            left = send.at[section, chunk, pl.ds(0, blocks - 1)]
            pltpu.make_async_copy(left, left, send_sem.at[section, chunk]).wait()


def on_device(sketch, leaf_maps, mix_maps):
    groups, blocks = lax.axis_size("grp"), lax.axis_size("blk")
    total_cols, rows_dev = sketch.shape
    own_cols = total_cols // groups
    pair = leaf_maps.shape[2]
    sub = pair // 2
    leaves = rows_dev // sub
    low = leaves // blocks
    rows = min(2 * TILE, own_cols)
    chunks = own_cols // rows
    big = blocks * TILE
    any_space = pl.BlockSpec(memory_space=pl.ANY)
    in_vmem = pl.BlockSpec(memory_space=pltpu.VMEM)
    dma = pltpu.SemaphoreType.DMA
    bf16 = jnp.bfloat16
    return pl.pallas_call(
        functools.partial(chain_kernel, groups, blocks),
        out_shape=jax.ShapeDtypeStruct((own_cols, rows_dev), bf16),
        in_specs=[any_space, in_vmem, in_vmem],
        out_specs=any_space,
        scratch_shapes=[
            pltpu.VMEM((chunks, rows, rows_dev), bf16),
            pltpu.VMEM((groups, chunks, blocks, rows, low * sub), bf16),
            pltpu.VMEM((groups - 1, chunks, blocks, rows, low * sub), bf16),
            pltpu.VMEM((leaves, rows, sub), bf16),
            pltpu.VMEM((groups, pair, pair), bf16),
            pltpu.VMEM((groups, low * blocks, blocks), bf16),
            pltpu.VMEM((low, big, big), bf16),
            dma((chunks,)),
            dma((groups, chunks)),
            dma((groups, chunks)),
            dma((groups,)), dma((groups,)), dma((groups,)), dma((groups,)),
        ],
        compiler_params=pltpu.CompilerParams(
            collective_id=0, has_side_effects=True, vmem_limit_bytes=48 * 1024 * 1024),
    )(sketch, leaf_maps.reshape(pair, pair), mix_maps.reshape(low * blocks, blocks))


def solution(mesh):
    placed = (P(None, "blk"), P("grp", "blk", None, None), P("grp", "blk", None, None))
    return jax.shard_map(
        on_device, mesh=mesh, in_specs=placed, out_specs=P("grp", "blk"), check_vma=False
    )
```

time: 161 us -> 105 us (0.65)
  Pallas kernels: 0 us -> 100 us
  waiting for transfers between devices: 94.8 us -> 0 us
  local copies, waits for them, and re-layouts: 38 us -> 2.94 us
  starting transfers between devices: 13.6 us -> 0 us
  blocking collectives: 8.13 us -> 0 us
  matrix products: 6.09 us -> 0 us
    pallas_call x0 -> x1, Pallas kernels: none -> 100 us  [on_device(): pl.pallas_call(functools.partial(chain_kernel, groups, blocks), out_shape...]
    all_to_all x2 -> x0, waiting for transfers between devices: 94.8 us -> none  [apply_section(): lax.all_to_all(result.reshape(columns, leaves, sub_rows), 'blk', split_ax...]
    all_to_all x2 -> x0, starting transfers between devices: 13.6 us -> none  [apply_section(): lax.all_to_all(result.reshape(columns, leaves, sub_rows), 'blk', split_ax...]
    reshape x5 -> x0, local copies, waits for them, and re-layouts: 12.6 us -> none  [the longest x2 5.09 us: apply_section(): paired = paired.reshape(columns, blocks, low_part, sub_rows)]
    convert_element_type x4 -> x0, local copies, waits for them, and re-layouts: 8.64 us -> none  [the longest x2 4.91 us: apply_section(): paired = jnp.dot(current.reshape(columns * leaves // 2, 2 * sub_rows), le...]
    all_gather x2 -> x0, blocking collectives: 8.13 us -> none  [the longest x1 4.68 us: on_device(): lax.all_gather(leaf_maps, 'grp', axis=0, tiled=True)]
    while x5 -> x0, local copies, waits for them, and re-layouts: 6.73 us -> none  [the longest x1 4.06 us: on_device(): current = lax.fori_loop(0, groups, advance_all, current)]
    dot_general x4 -> x0, matrix products: 6.09 us -> none  [the longest x2 4.71 us: apply_section(): jnp.dot(current.reshape(columns * leaves // 2, 2 * sub_rows), leaf_map, p...]
  transfers between devices with their start and end apart: 2 -> 0, of which waited for: 2 -> 0; matrix products, arithmetic and copies ran while one was open for 0% -> 0% of each run, Pallas kernels for 0% -> 0%
where the time goes in v1:
time: 105 us; the launch traced here: 103 us
  Pallas kernels  100 us (95%)
  local copies, waits for them, and re-layouts  2.94 us (3%)
    pallas_call x1, Pallas kernels, on_device(): pl.pallas_call(functools.partial(chain_kernel, groups, blocks), out_shape...  100 us
    unnamed x5, local copies, waits for them, and re-layouts  2.94 us

profile of v1, /device:TPU:15, one launch (start us, length us, event | category | flops | bytes accessed | tf_op | source)
XLA Modules:
  0.0 103.3 jit_solution(14963989195759464125)
XLA Ops:
  0.0 0.0 copy-start
  0.0 0.9 copy-done
  0.9 0.0 copy-start.1
  0.9 0.7 copy-done.1
  1.6 100.4 %shard_map.37 = bf16[128,8192]{1,0:T(8,128)(2,1)S(1)} custom-call(bf16[256,8192]{1,0:T(8,128)(2,1)} %sketch_ref.1, bf16[256,256]{1,0:T(8,128)(2,1)S(1)} %bitcast.2, bf16[64,16]{1,0:T(8,128)(2,1)S(1)} %bitcast.3), custom_call_target="tpu_custom_call" | custom-call | tf_op jit(solution)/shard_map/pallas_call | solution.py:170
  102.0 1.3 %copy.5 = bf16[128,8192]{1,0:T(8,128)(2,1)} copy(bf16[128,8192]{1,0:T(8,128)(2,1)S(1)} %shard_map.37) | data formatting | bytes 4194304
Async XLA Ops:
  0.0 0.9 copy-start
  0.9 0.7 copy-start.1

commit v2 on v0

v2 whole, which is shorter than its diff:
```python
import functools

import jax
import jax.numpy as jnp
from jax import lax
from jax.experimental import pallas as pl
from jax.experimental.pallas import tpu as pltpu
from jax.sharding import PartitionSpec as P

MESH = pl.DeviceIdType.MESH
TILE = 16
LANES = 128


def chunk_rows(own_cols):
    left, sizes = own_cols, []
    for size in CHUNKS:
        if left >= size:
            sizes.append(size)
            left -= size
    while left > 0:
        sizes.append(min(left, 2 * TILE))
        left -= sizes[-1]
    return sizes


CHUNKS = (16,16,32,64)


def chain_kernel(
    groups, blocks, sizes, sketch_ref, leaf_in, mix_in, out_ref,
    x_vm, send, recv, half, leaf_all, mix_vm, mix_all, weights,
    x_sem, send_sem, recv_sem, own_sem, leaf_send, leaf_recv, mix_send, mix_recv, go_sem,
):
    grp = lax.axis_index("grp")
    blk = lax.axis_index("blk")
    own_cols, row_len = x_vm.shape
    sub = leaf_in.shape[0] // 2
    leaves = row_len // sub
    low = leaves // blocks
    wide = low * sub
    starts = [sum(sizes[:i]) for i in range(len(sizes))]
    big = blocks * TILE

    barrier = pltpu.get_barrier_semaphore()

    def greet(**where):
        pl.semaphore_signal(barrier, inc=1, device_id=where, device_id_type=MESH)

    @pl.when(grp == 0)
    def _():
        for step in range(blocks):
            greet(grp=1, blk=lax.rem(blk + step, blocks))
        for other in range(2, groups):
            greet(grp=other, blk=blk)

    @pl.when(grp > 0)
    def _():
        for step in range(1, groups):
            greet(grp=lax.rem(grp + step, groups), blk=blk)
        for step in range(1, blocks):
            greet(grp=grp, blk=lax.rem(blk + step, blocks))

    own_mix = pltpu.make_async_copy(mix_in, mix_vm, own_sem.at[0])
    own_leaf = pltpu.make_async_copy(leaf_in, leaf_all.at[grp], own_sem.at[1])
    own_mix.start()
    own_leaf.start()

    def load(chunk):
        rows = pl.ds(pl.multiple_of(grp * own_cols + starts[chunk], TILE), sizes[chunk])
        return pltpu.make_async_copy(
            sketch_ref.at[rows, :], x_vm.at[pl.ds(starts[chunk], sizes[chunk]), :], x_sem.at[chunk])

    for chunk in range(len(sizes)):
        load(chunk).start()

    own_mix.wait()
    pick = (
        lax.broadcasted_iota(jnp.int32, (blocks, blocks), 0)
        == lax.broadcasted_iota(jnp.int32, (blocks, blocks), 1)
    ).astype(jnp.bfloat16)
    mix_all[grp] = jnp.zeros(mix_all.shape[1:], jnp.bfloat16)
    mix_all[grp, :, pl.ds(0, low * blocks)] = lax.dot_general(
        pick, mix_vm[...], (((1,), (1,)), ((), ())), preferred_element_type=jnp.float32
    ).astype(jnp.bfloat16)
    own_leaf.wait()

    def factor_copies(target, owner):
        where = {"grp": target}
        return (
            pltpu.make_async_remote_copy(
                leaf_in, leaf_all.at[owner], leaf_send.at[target], leaf_recv.at[owner],
                device_id=where, device_id_type=MESH),
            pltpu.make_async_remote_copy(
                mix_all.at[owner], mix_all.at[owner], mix_send.at[target], mix_recv.at[owner],
                device_id=where, device_id_type=MESH),
        )

    def send_factors():
        for step in range(1, groups):
            for copy in factor_copies(lax.rem(grp + step, groups), grp):
                copy.start()

    @pl.when(grp == 0)
    def _():
        pl.semaphore_wait(barrier, groups - 1)
        send_factors()

    @pl.when(grp == 1)
    def _():
        pl.semaphore_wait(barrier, 2 * blocks - 1 + groups - 2)
        pl.semaphore_signal(go_sem, inc=1, device_id={"grp": 0}, device_id_type=MESH)
        send_factors()

    @pl.when(grp > 1)
    def _():
        pl.semaphore_wait(barrier, blocks - 1 + groups - 1)
        send_factors()

    spread = (
        lax.broadcasted_iota(jnp.int32, (big, blocks), 0) // TILE
        == lax.broadcasted_iota(jnp.int32, (big, blocks), 1)
    ).astype(jnp.bfloat16)
    same = (
        lax.broadcasted_iota(jnp.int32, (big, big), 0) % TILE
        == lax.broadcasted_iota(jnp.int32, (big, big), 1) % TILE
    )
    nums = (((1,), (1,)), ((), ()))
    width = mix_all.shape[2]

    def build_weights(section):
        for l in range(low):
            chosen = (
                lax.broadcasted_iota(jnp.int32, (big, width), 0) // TILE + l * blocks
                == lax.broadcasted_iota(jnp.int32, (big, width), 1)
            ).astype(jnp.bfloat16)
            tall = lax.dot_general(
                chosen, mix_all[section], nums, preferred_element_type=jnp.float32
            ).astype(jnp.bfloat16)
            full = lax.dot_general(tall, spread, nums, preferred_element_type=jnp.float32)
            weights[l] = jnp.where(same, full, 0.0).astype(jnp.bfloat16)

    def compute(section, start, rows):
        unit = pl.ds(start, rows)
        tiles = rows // TILE

        def piece(leaf):
            if section == 0:
                return x_vm[unit, pl.ds(leaf * sub, sub)]
            return recv[section - 1, leaf // low, unit, pl.ds(leaf % low * sub, sub)]

        leaf_map = leaf_all[section]
        per = min(leaves // 2, max(1, 256 // rows))
        for first in range(0, leaves // 2, per):
            lhs = jnp.concatenate(
                [jnp.concatenate([piece(2 * m), piece(2 * m + 1)], axis=1)
                 for m in range(first, first + per)], axis=0)
            product = jnp.dot(
                lhs, leaf_map, preferred_element_type=jnp.float32).astype(jnp.bfloat16)
            for i in range(per):
                for j in range(2):
                    half[2 * (first + i) + j, pl.ds(0, rows), :] = product[
                        i * rows:(i + 1) * rows, j * sub:(j + 1) * sub]

        for l in range(low):
            rhs = jnp.concatenate(
                [jnp.concatenate(
                    [half[k * low + l, pl.ds(t * TILE, TILE), :] for t in range(tiles)], axis=1)
                 for k in range(blocks)], axis=0)
            mixed = jnp.dot(
                weights[l], rhs, preferred_element_type=jnp.float32).astype(jnp.bfloat16)
            for h in range(blocks):
                for t in range(tiles):
                    send[section, h, pl.ds(start + t * TILE, TILE), pl.ds(l * sub, sub)] = mixed[
                        h * TILE:(h + 1) * TILE, t * sub:(t + 1) * sub]

    order = sorted(range(1, blocks), key=lambda step: (abs(step - blocks // 2), step))

    for section in range(groups):
        @pl.when(grp != section)
        def _():
            for copy in factor_copies(section, section):
                copy.wait_recv()

        build_weights(section)

        for chunk, (start, rows) in enumerate(zip(starts, sizes)):
            span = pl.ds(start, rows)
            if section == 0:
                load(chunk).wait()
            else:
                arrived = recv.at[section - 1, :, span, :]
                pltpu.make_async_copy(arrived, arrived, recv_sem.at[section - 1, chunk]).wait()

            unit = half.shape[1]
            if rows <= unit:
                compute(section, start, rows)
            else:
                @pl.loop(0, rows // unit)
                def _(i):
                    compute(section, pl.multiple_of(start + i * unit, TILE), unit)

            if section == 0 and chunk == 0:
                @pl.when(grp == 0)
                def _():
                    pl.semaphore_wait(go_sem, 1)

            if section == groups - 1:
                place = out_ref.at[span, pl.ds(pl.multiple_of(blk * wide, sub), wide)]
            else:
                place = recv.at[section, blk, span, :]
            for step in order:
                target = lax.rem(blk + step, blocks)
                pltpu.make_async_remote_copy(
                    send.at[section, target, span, :], place,
                    send_sem.at[section, chunk], recv_sem.at[section, chunk],
                    device_id={"blk": target}, device_id_type=MESH).start()
            pltpu.make_async_copy(
                send.at[section, blk, span, :], place, recv_sem.at[section, chunk]).start()

    for step in range(1, groups):
        for copy in factor_copies(lax.rem(grp + step, groups), grp):
            copy.wait_send()
    for chunk, (start, rows) in enumerate(zip(starts, sizes)):
        span = pl.ds(start, rows)
        for section in range(groups):
            left = send.at[section, pl.ds(0, blocks - 1), span, :]
            pltpu.make_async_copy(left, left, send_sem.at[section, chunk]).wait()
        arrived = out_ref.at[span, :]
        pltpu.make_async_copy(arrived, arrived, recv_sem.at[groups - 1, chunk]).wait()


def on_device(sketch, leaf_maps, mix_maps):
    groups, blocks = lax.axis_size("grp"), lax.axis_size("blk")
    total_cols, rows_dev = sketch.shape
    own_cols = total_cols // groups
    pair = leaf_maps.shape[2]
    sub = pair // 2
    leaves = rows_dev // sub
    low = leaves // blocks
    sizes = chunk_rows(own_cols)
    big = blocks * TILE
    width = -(-low * blocks // LANES) * LANES
    in_hbm = pl.BlockSpec(memory_space=pltpu.HBM)
    dma = pltpu.SemaphoreType.DMA
    bf16 = jnp.bfloat16
    return pl.pallas_call(
        functools.partial(chain_kernel, groups, blocks, sizes),
        out_shape=jax.ShapeDtypeStruct((own_cols, rows_dev), bf16),
        in_specs=[in_hbm, in_hbm, in_hbm],
        out_specs=pl.BlockSpec(memory_space=pl.ANY),
        scratch_shapes=[
            pltpu.VMEM((own_cols, rows_dev), bf16),
            pltpu.VMEM((groups, blocks, own_cols, low * sub), bf16),
            pltpu.VMEM((groups - 1, blocks, own_cols, low * sub), bf16),
            pltpu.VMEM((leaves, 2 * TILE, sub), bf16),
            pltpu.VMEM((groups, pair, pair), bf16),
            pltpu.VMEM((low * blocks, blocks), bf16),
            pltpu.VMEM((groups, blocks, width), bf16),
            pltpu.VMEM((low, big, big), bf16),
            dma((len(sizes),)),
            dma((groups, len(sizes))),
            dma((groups, len(sizes))),
            dma((2,)),
            dma((groups,)), dma((groups,)), dma((groups,)), dma((groups,)),
            pltpu.SemaphoreType.REGULAR,
        ],
        compiler_params=pltpu.CompilerParams(
            collective_id=0, has_side_effects=True, vmem_limit_bytes=48 * 1024 * 1024),
    )(sketch, leaf_maps.reshape(pair, pair), mix_maps.reshape(low * blocks, blocks))


def solution(mesh):
    placed = (P(None, "blk"), P("grp", "blk", None, None), P("grp", "blk", None, None))
    return jax.shard_map(
        on_device, mesh=mesh, in_specs=placed, out_specs=P("grp", "blk"), check_vma=False
    )
```

time: 161 us -> 102 us (0.63)
  Pallas kernels: 0 us -> 98.5 us
  waiting for transfers between devices: 94.8 us -> 0 us
  local copies, waits for them, and re-layouts: 38 us -> 2.94 us
  starting transfers between devices: 13.6 us -> 0 us
  blocking collectives: 8.13 us -> 0 us
  matrix products: 6.09 us -> 0 us
    pallas_call x0 -> x1, Pallas kernels: none -> 98.5 us  [on_device(): pl.pallas_call(functools.partial(chain_kernel, groups, blocks, sizes), ou...]
    all_to_all x2 -> x0, waiting for transfers between devices: 94.8 us -> none  [apply_section(): lax.all_to_all(result.reshape(columns, leaves, sub_rows), 'blk', split_ax...]
    all_to_all x2 -> x0, starting transfers between devices: 13.6 us -> none  [apply_section(): lax.all_to_all(result.reshape(columns, leaves, sub_rows), 'blk', split_ax...]
    reshape x5 -> x0, local copies, waits for them, and re-layouts: 12.6 us -> none  [the longest x2 5.09 us: apply_section(): paired = paired.reshape(columns, blocks, low_part, sub_rows)]
    convert_element_type x4 -> x0, local copies, waits for them, and re-layouts: 8.64 us -> none  [the longest x2 4.91 us: apply_section(): paired = jnp.dot(current.reshape(columns * leaves // 2, 2 * sub_rows), le...]
    all_gather x2 -> x0, blocking collectives: 8.13 us -> none  [the longest x1 4.68 us: on_device(): lax.all_gather(leaf_maps, 'grp', axis=0, tiled=True)]
    while x5 -> x0, local copies, waits for them, and re-layouts: 6.73 us -> none  [the longest x1 4.06 us: on_device(): current = lax.fori_loop(0, groups, advance_all, current)]
    dot_general x4 -> x0, matrix products: 6.09 us -> none  [the longest x2 4.71 us: apply_section(): jnp.dot(current.reshape(columns * leaves // 2, 2 * sub_rows), leaf_map, p...]
  transfers between devices with their start and end apart: 2 -> 0, of which waited for: 2 -> 0; matrix products, arithmetic and copies ran while one was open for 0% -> 0% of each run, Pallas kernels for 0% -> 0%
where the time goes in v2:
time: 102 us; the launch traced here: 101 us
  Pallas kernels  98.5 us (97%)
  local copies, waits for them, and re-layouts  2.94 us (3%)
    pallas_call x1, Pallas kernels, on_device(): pl.pallas_call(functools.partial(chain_kernel, groups, blocks, sizes), ou...  98.5 us
    unnamed x5, local copies, waits for them, and re-layouts  2.94 us

profile of v2, /device:TPU:15, one launch (start us, length us, event | category | flops | bytes accessed | tf_op | source)
XLA Modules:
  0.0 101.5 jit_solution(11327300720362784271)
XLA Ops:
  0.0 0.0 copy-start
  0.0 0.9 copy-done
  0.9 0.0 copy-start.1
  0.9 0.7 copy-done.1
  1.6 98.5 %shard_map.37 = bf16[128,8192]{1,0:T(8,128)(2,1)S(1)} custom-call(bf16[256,8192]{1,0:T(8,128)(2,1)} %sketch_ref.1, bf16[256,256]{1,0:T(8,128)(2,1)S(1)} %bitcast.2, bf16[64,16]{1,0:T(8,128)(2,1)S(1)} %bitcast.3), custom_call_target="tpu_custom_call" | custom-call | tf_op jit(solution)/shard_map/pallas_call | solution.py:247
  100.2 1.3 %copy.5 = bf16[128,8192]{1,0:T(8,128)(2,1)} copy(bf16[128,8192]{1,0:T(8,128)(2,1)S(1)} %shard_map.37) | data formatting | bytes 4194304
Async XLA Ops:
  0.0 0.9 copy-start
  0.9 0.7 copy-start.1

commit v3 on v2

--- a/solution.py
+++ b/solution.py
@@ -83,16 +83,14 @@
     mix_all[grp, :, pl.ds(0, low * blocks)] = lax.dot_general(
         pick, mix_vm[...], (((1,), (1,)), ((), ())), preferred_element_type=jnp.float32
     ).astype(jnp.bfloat16)
-    own_leaf.wait()
-
     def factor_copies(target, owner):
         where = {"grp": target}
         return (
             pltpu.make_async_remote_copy(
-                leaf_in, leaf_all.at[owner], leaf_send.at[target], leaf_recv.at[owner],
+                mix_all.at[owner], mix_all.at[owner], mix_send.at[target], mix_recv.at[owner],
                 device_id=where, device_id_type=MESH),
             pltpu.make_async_remote_copy(
-                mix_all.at[owner], mix_all.at[owner], mix_send.at[target], mix_recv.at[owner],
+                leaf_in, leaf_all.at[owner], leaf_send.at[target], leaf_recv.at[owner],
                 device_id=where, device_id_type=MESH),
         )
 
@@ -110,12 +108,10 @@
     def _():
         pl.semaphore_wait(barrier, 2 * blocks - 1 + groups - 2)
         pl.semaphore_signal(go_sem, inc=1, device_id={"grp": 0}, device_id_type=MESH)
-        send_factors()
 
     @pl.when(grp > 1)
     def _():
         pl.semaphore_wait(barrier, blocks - 1 + groups - 1)
-        send_factors()
 
     spread = (
         lax.broadcasted_iota(jnp.int32, (big, blocks), 0) // TILE
@@ -174,15 +170,22 @@
                     send[section, h, pl.ds(start + t * TILE, TILE), pl.ds(l * sub, sub)] = mixed[
                         h * TILE:(h + 1) * TILE, t * sub:(t + 1) * sub]
 
-    order = sorted(range(1, blocks), key=lambda step: (abs(step - blocks // 2), step))
+    order = list(range(1, blocks))
 
     for section in range(groups):
         @pl.when(grp != section)
         def _():
-            for copy in factor_copies(section, section):
-                copy.wait_recv()
+            factor_copies(section, section)[0].wait_recv()
 
         build_weights(section)
+
+        @pl.when(grp != section)
+        def _():
+            factor_copies(section, section)[1].wait_recv()
+
+        @pl.when(grp == section)
+        def _():
+            own_leaf.wait()
 
         for chunk, (start, rows) in enumerate(zip(starts, sizes)):
             span = pl.ds(start, rows)
@@ -204,6 +207,10 @@
                 @pl.when(grp == 0)
                 def _():
                     pl.semaphore_wait(go_sem, 1)
+
+                @pl.when(grp > 0)
+                def _():
+                    send_factors()
 
             if section == groups - 1:
                 place = out_ref.at[span, pl.ds(pl.multiple_of(blk * wide, sub), wide)]

time: 102 us -> 101 us (level)
  no operation moved by 1% of the time
where the time goes in v3:
time: 101 us
  Pallas kernels  97.6 us (97%)
  local copies, waits for them, and re-layouts  2.94 us (3%)
    pallas_call x1, Pallas kernels, on_device(): pl.pallas_call(functools.partial(chain_kernel, groups, blocks, sizes), ou...  97.6 us
    unnamed x5, local copies, waits for them, and re-layouts  2.94 us

profile of v3, /device:TPU:15, one launch (start us, length us, event | category | flops | bytes accessed | tf_op | source)
XLA Modules:
  0.0 100.5 jit_solution(1152516679166331870)
XLA Ops:
  0.0 0.0 copy-start
  0.0 0.9 copy-done
  0.9 0.0 copy-start.1
  0.9 0.7 copy-done.1
  1.6 97.6 %shard_map.37 = bf16[128,8192]{1,0:T(8,128)(2,1)S(1)} custom-call(bf16[256,8192]{1,0:T(8,128)(2,1)} %sketch_ref.1, bf16[256,256]{1,0:T(8,128)(2,1)S(1)} %bitcast.2, bf16[64,16]{1,0:T(8,128)(2,1)S(1)} %bitcast.3), custom_call_target="tpu_custom_call" | custom-call | tf_op jit(solution)/shard_map/pallas_call | solution.py:254
  99.2 1.3 %copy.5 = bf16[128,8192]{1,0:T(8,128)(2,1)} copy(bf16[128,8192]{1,0:T(8,128)(2,1)S(1)} %shard_map.37) | data formatting | bytes 4194304
Async XLA Ops:
  0.0 0.9 copy-start
  0.9 0.7 copy-start.1
